TPU v7x, 32 devices: a whole 2x2x4 slice. The times are simulated.
32 devices in a mesh: groups: 2 (over x), ctx: 8 (over z, y), head: 2 (over core).
Axes of the slice: x: 2, y: 2, z: 4, core: 2. Of those that a mesh axis runs over, the one named last changes fastest.
Arguments:
- queries: bfloat16 [4096, 2048], P(('groups', 'ctx'), 'head'), parts along dimension 0, may hold values from -180 to 180
- keys: bfloat16 [4096, 2048], P(('groups', 'ctx'), 'head'), parts along dimension 0, may hold values from -6 to 6
- values: bfloat16 [4096, 2048], P(('groups', 'ctx'), 'head'), parts along dimension 0, may hold values from -6 to 6
- out_weight: bfloat16 [2048, 2048], P(None, 'head'), may hold values from -0.125 to 0.125
- random_blocks: int32 [32, 3], P('groups'), parts along dimension 0, may hold values from 0 to 15, as said below
- window_blocks: int32 [32], P(('groups', 'ctx')), parts along dimension 0, may hold values from 0 to 1
- global_blocks: int32 [4], P('groups'), parts along dimension 0, may hold values from 0 to 15, as said below
Outputs:
- layer_out: bfloat16 [4096, 2048], P(('groups', 'ctx'), 'head'), parts along dimension 0
There are 2 independent parts, one for each index of `groups`. A program takes and returns all parts, laid end to end along the dimension named above; an argument that names none is the same for every part. Nothing has to cross between parts.
Inputs may be any that keep to these rules, and one draw needn't show every extreme that they name: `random_blocks`: the random blocks named in the rows of one index j of ctx (rows j * 2 to j * 2 + 1) lie outside blocks j * 2 to j * 2 + 1; counted with repeats, at most 1 of them lie in the blocks k * 2 to k * 2 + 1 of any one other index k, and exactly 1 for some k. `global_blocks`: 2 different block numbers.
All inputs are finite; a program needn't handle non-finite values.
Results may differ from a plain program's by a relative error of at most 0.0055.
Values may be sent and summed in bfloat16 or wider, within the bound.
A program may use at most 128 MiB of HBM per device.

v0:
```python
import math
import jax
import jax.numpy as jnp
from jax import lax
from jax.sharding import PartitionSpec as P

HEAD = 128
BLOCK = 128
WMAX = 1
GLOB = 2
RAND = 3
LARGE_NEG = -1e30


def with_halo(block, sides, width):
    for axis, dim in sides:
        count = lax.axis_size(axis)
        forward = [(i, i + 1) for i in range(count - 1)]
        backward = [(target, source) for source, target in forward]
        low = lax.ppermute(
            lax.slice_in_dim(block, block.shape[dim] - width, None, axis=dim), axis, forward
        )
        high = lax.ppermute(lax.slice_in_dim(block, 0, width, axis=dim), axis, backward)
        block = jnp.concatenate([low, block, high], axis=dim)
    return block


def split_heads(tensor):
    return tensor.reshape(tensor.shape[:-1] + (tensor.shape[-1] // HEAD, HEAD))


def block_partial(query_rows, key_rows, value_rows):
    query_heads = split_heads(query_rows)
    key_heads = split_heads(key_rows)
    value_heads = split_heads(value_rows)
    scores = jnp.einsum(
        "gqhd,gckhd->gchqk", query_heads, key_heads, preferred_element_type=jnp.float32
    ) * (1.0 / math.sqrt(HEAD))
    row_peak = jnp.max(scores, axis=-1)
    weights = jnp.exp(scores - row_peak[..., None])
    row_total = jnp.sum(weights, axis=-1)
    partial_out = jnp.einsum(
        "gchqk,gckhd->gcqhd",
        weights.astype(jnp.bfloat16),
        value_heads,
        preferred_element_type=jnp.float32,
    )
    partial_out = partial_out.reshape(partial_out.shape[:-2] + (-1,))
    return (partial_out, jnp.swapaxes(row_peak, -1, -2), jnp.swapaxes(row_total, -1, -2))


def combine(partial_out, row_peak, row_total, used_flags):
    used_mask = used_flags[:, :, None, None]
    best_peak = jnp.max(jnp.where(used_mask, row_peak, LARGE_NEG), axis=1, keepdims=True)
    factor = jnp.where(used_mask, jnp.exp(row_peak - best_peak), 0.0)
    weighted = jnp.sum(split_heads(partial_out) * factor[..., None], axis=1)
    normalizer = jnp.sum(row_total * factor, axis=1)
    result = weighted / normalizer[..., None]
    return result.reshape(result.shape[:-2] + (-1,))


def candidates(first_block, block_count, widths, global_ids, random_rows, total_blocks):
    query_ids = first_block + jnp.arange(block_count, dtype=jnp.int32)
    offsets = jnp.arange(-WMAX, WMAX + 1, dtype=jnp.int32)
    window_ids = query_ids[:, None] + offsets[None, :]
    window_valid = (
        (jnp.abs(offsets)[None, :] <= widths[:, None])
        & (window_ids >= 0)
        & (window_ids < total_blocks)
    )
    global_rows = jnp.broadcast_to(global_ids[None, :], (block_count, GLOB))
    block_ids = jnp.concatenate([window_ids, global_rows, random_rows], axis=1)
    valid = jnp.concatenate(
        [window_valid, jnp.ones((block_count, GLOB + RAND), dtype=bool)], axis=1
    )
    width_all = block_ids.shape[1]
    same_block = block_ids[:, :, None] == block_ids[:, None, :]
    earlier = jnp.arange(width_all)[None, :] < jnp.arange(width_all)[:, None]
    shadowed = jnp.any(same_block & valid[:, None, :] & earlier[None, :, :], axis=2)
    return (block_ids, valid & jnp.logical_not(shadowed))


def per_device(queries, keys, values, out_weight, random_blocks, window_blocks, global_blocks):
    ctx_count = lax.axis_size("ctx")
    position = lax.axis_index("ctx")
    tok_rows, row_width = queries.shape
    dev_blocks = tok_rows // BLOCK
    total_blocks = dev_blocks * ctx_count
    requests = dev_blocks * RAND
    capacity = (requests + ctx_count - 2) // (ctx_count - 1)
    first_block = position * dev_blocks
    key_value = jnp.stack([keys, values])
    own_blocks = key_value.reshape(2, dev_blocks, BLOCK, row_width)
    extended = with_halo(key_value, (("ctx", 1),), WMAX * BLOCK)
    rim_blocks = extended.reshape(2, dev_blocks + 2 * WMAX, BLOCK, row_width)
    global_owner = global_blocks // dev_blocks
    global_slot = global_blocks % dev_blocks
    picked = jnp.take(own_blocks, global_slot, axis=1)
    owned_here = (global_owner == position)[None, :, None, None]
    global_terms = jnp.where(owned_here, picked.astype(jnp.float32), 0.0)
    global_pairs = lax.psum(global_terms.astype(jnp.bfloat16), "ctx")
    request_table = random_blocks.reshape(ctx_count, requests)
    owners = request_table // dev_blocks
    within = request_table % dev_blocks
    same_owner = owners[:, :, None] == owners[:, None, :]
    before = jnp.arange(requests)[None, :] < jnp.arange(requests)[:, None]
    rank_table = jnp.sum(same_owner & before[None, :, :], axis=2)
    slot_ids = jnp.arange(capacity, dtype=jnp.int32)
    toward_me = (owners == position)[:, :, None] & (
        rank_table[:, :, None] == slot_ids[None, None, :]
    )
    send_index = jnp.sum(jnp.where(toward_me, within[:, :, None], 0), axis=1)
    my_owner = lax.dynamic_index_in_dim(owners, position, 0, keepdims=False)
    my_rank = lax.dynamic_index_in_dim(rank_table, position, 0, keepdims=False)
    my_slot = my_owner * capacity + my_rank
    my_random = lax.dynamic_slice_in_dim(random_blocks, first_block, dev_blocks, 0)
    block_ids, used_flags = candidates(
        first_block, dev_blocks, window_blocks, global_blocks, my_random, total_blocks
    )
    window_index = (
        jnp.arange(dev_blocks, dtype=jnp.int32)[:, None]
        + WMAX
        + jnp.arange(-WMAX, WMAX + 1, dtype=jnp.int32)[None, :]
    )
    global_index = jnp.broadcast_to(
        dev_blocks + 2 * WMAX + jnp.arange(GLOB, dtype=jnp.int32)[None, :], (dev_blocks, GLOB)
    )
    local_pool = jnp.concatenate([rim_blocks, global_pairs], axis=1)
    query_blocks = queries.reshape(dev_blocks, BLOCK, row_width)
    slot_hits = (my_owner[:, None, None] == jnp.arange(ctx_count)[None, :, None]) & (
        my_rank[:, None, None] == slot_ids[None, None, :]
    )
    query_pick = jnp.sum(
        jnp.where(slot_hits, (jnp.arange(requests) // RAND)[:, None, None], 0), axis=0
    )
    outgoing = jnp.take(query_blocks, query_pick, axis=0)
    arrived = lax.all_to_all(outgoing, "ctx", split_axis=0, concat_axis=0, tiled=True)
    item_rows = arrived.shape[2]
    partners = jnp.take(own_blocks, send_index, axis=1)
    flat_queries = arrived.reshape(ctx_count * capacity, item_rows, row_width)
    part_out, part_peak, part_total = block_partial(flat_queries, partners[0], partners[1])
    back_out = lax.all_to_all(part_out, "ctx", split_axis=0, concat_axis=0, tiled=True)
    back_peak = lax.all_to_all(part_peak, "ctx", split_axis=0, concat_axis=0, tiled=True)
    back_total = lax.all_to_all(part_total, "ctx", split_axis=0, concat_axis=0, tiled=True)
    head_count = back_peak.shape[-1]
    rand_out = back_out.reshape(ctx_count * capacity, BLOCK, row_width)[my_slot].reshape(
        dev_blocks, RAND, BLOCK, row_width
    )
    rand_peak = back_peak.reshape(ctx_count * capacity, BLOCK, head_count)[my_slot].reshape(
        dev_blocks, RAND, BLOCK, head_count
    )
    rand_total = back_total.reshape(ctx_count * capacity, BLOCK, head_count)[my_slot].reshape(
        dev_blocks, RAND, BLOCK, head_count
    )
    pool_index = jnp.concatenate([window_index, global_index], axis=1)
    remote_parts = (rand_out, rand_peak, rand_total)
    group_size = math.gcd(dev_blocks, max(1, 512 // BLOCK))
    steps_count = dev_blocks // group_size

    def regroup(tensor):
        return tensor.reshape((steps_count, group_size) + tensor.shape[1:])

    def attend(inputs):
        query_group, index_group, used_group, extra_group = inputs
        gathered = jnp.take(local_pool, index_group, axis=1)
        part_out, part_peak, part_total = block_partial(query_group, gathered[0], gathered[1])
        part_out = jnp.concatenate([part_out, extra_group[0]], axis=1)
        part_peak = jnp.concatenate([part_peak, extra_group[1]], axis=1)
        part_total = jnp.concatenate([part_total, extra_group[2]], axis=1)
        return combine(part_out, part_peak, part_total, used_group).astype(jnp.bfloat16)

    extra_groups = tuple((regroup(member) for member in remote_parts))
    attended = lax.map(
        attend, (regroup(query_blocks), regroup(pool_index), regroup(used_flags), extra_groups)
    )
    attended = attended.reshape(tok_rows, row_width)
    layer_sum = jnp.dot(
        lax.all_gather(attended, "head", axis=1, tiled=True),
        out_weight,
        preferred_element_type=jnp.float32,
    )
    return layer_sum.astype(jnp.bfloat16)


def solution(mesh):
    placed = (
        P(("groups", "ctx"), "head"),
        P(("groups", "ctx"), "head"),
        P(("groups", "ctx"), "head"),
        P(None, "head"),
        P("groups", None),
        P(("groups", "ctx")),
        P("groups"),
    )
    return jax.shard_map(
        per_device,
        mesh=mesh,
        in_specs=placed,
        out_specs=P(("groups", "ctx"), "head"),
        check_vma=False,
    )
```

profile of v0, /device:TPU:0, one launch (start us, length us, event | category | flops | bytes accessed | tf_op | source)
XLA Modules:
  0.0 301.7 jit_solution(17253878951724094730)
XLA Ops:
  8.4 1.7 gather_fusion.3
  10.1 1.6 fusion.18
  11.7 7.3 %all-to-all-start = ((bf16[8,1,128,1024]{3,2,1,0:T(8,128)(2,1)}), bf16[8,1,128,1024]{3,2,1,0:T(8,128)(2,1)}, u32[]{:S(2)}, u32[]{:S(2)}) async-start(bf16[8,1,128,1024]{3,2,1,0:T(8,128)(2,1)} %fusion.18), calls=%async_computation | async-start | bytes 4194304 | tf_op jit(solution)/shard_map/all_to_all | solution.py:137
  19.7 2.7 gather_fusion.2
  22.5 2.7 bitcast_select_fusion
  25.1 1.8 fusion.48
  26.9 2.4 copy.198
  29.3 3.0 %copy.197 = bf16[1,8,1,128,1024]{3,4,1,2,0:T(8,128)(2,1)S(1)} copy(bf16[1,8,1,128,1024]{4,3,0,1,2:T(8,128)(2,1)} %get-tuple-element.41) | data formatting | bytes 4194304 | tf_op jit(solution)/shard_map/slice | solution.py:141
  32.4 35.0 %all-to-all-done = bf16[8,1,128,1024]{3,2,1,0:T(8,128)(2,1)} async-done(((bf16[8,1,128,1024]{3,2,1,0:T(8,128)(2,1)}), bf16[8,1,128,1024]{3,2,1,0:T(8,128)(2,1)}, u32[]{:S(2)}, u32[]{:S(2)}) %all-to-all-start) | async-done | bytes 2097184 | tf_op jit(solution)/shard_map/all_to_all | solution.py:137
  67.4 3.9 %copy.200 = bf16[8,1,128,1024]{2,3,0,1:T(8,128)(2,1)} copy(bf16[8,1,128,1024]{3,2,1,0:T(8,128)(2,1)} %all-to-all-done) | data formatting | bytes 4194304 | tf_op jit(solution)/shard_map/all_to_all | solution.py:137
  71.3 5.7 %bitcast_reduce_fusion.1 = (f32[8,8,128]{2,1,0:T(8,128)}, f32[8,8,128,128]{3,2,1,0:T(8,128)}) fusion(bf16[8,128,8,128]{1,3,2,0:T(8,128)(2,1)} %bitcast.118, bf16[8,128,8,128]{1,3,2,0:T(8,128)(2,1)} %bitcast.119), kind=kOutput, calls=%fused_computation.18 | convolution fusion | flops 270524416 | bytes 8421376 | tf_op jit(solution)/shard_map/gqhd,gckhd->gchqk/dot_general | solution.py:36
  77.0 3.6 %all-to-all-start.2 = ((f32[8,1,128,8]{2,3,1,0:T(8,128)}), f32[8,1,128,8]{2,3,1,0:T(8,128)S(1)}, u32[]{:S(2)}, u32[]{:S(2)}) async-start(f32[8,1,128,8]{2,3,1,0:T(8,128)} %bitcast.39), calls=%async_computation.2 | async-start | bytes 65536 | tf_op jit(solution)/shard_map/all_to_all | solution.py:143
  80.6 3.7 %fusion.6 = f32[8,8,128]{2,1,0:T(8,128)} fusion(f32[8,8,128,128]{3,2,1,0:T(8,128)} %get-tuple-element.49, f32[8,8,128]{2,1,0:T(8,128)} %get-tuple-element.48), kind=kLoop, calls=%fused_computation.20 | loop fusion | flops 3137536 | bytes 4259840 | tf_op jit(solution)/shard_map/reduce_sum | solution.py:41
  84.3 3.0 %all-to-all-done.2 = f32[8,1,128,8]{2,3,1,0:T(8,128)S(1)} async-done(((f32[8,1,128,8]{2,3,1,0:T(8,128)}), f32[8,1,128,8]{2,3,1,0:T(8,128)S(1)}, u32[]{:S(2)}, u32[]{:S(2)}) %all-to-all-start.2) | async-done | bytes 32800 | tf_op jit(solution)/shard_map/all_to_all | solution.py:143
  87.3 3.3 %all-to-all-start.3 = ((f32[8,1,128,8]{2,3,1,0:T(8,128)}), f32[8,1,128,8]{2,3,1,0:T(8,128)S(1)}, u32[]{:S(2)}, u32[]{:S(2)}) async-start(f32[8,1,128,8]{2,3,1,0:T(8,128)} %bitcast.44), calls=%async_computation.3 | async-start | bytes 65536 | tf_op jit(solution)/shard_map/all_to_all | solution.py:144
  90.6 5.1 %fusion.16 = f32[8,8,128,128]{3,2,1,0:T(8,128)} fusion(bf16[8,128,8,128]{1,3,2,0:T(8,128)(2,1)S(1)} %bitcast.116, f32[8,8,128,128]{3,2,1,0:T(8,128)} %get-tuple-element.49, f32[8,8,128]{2,1,0:T(8,128)} %get-tuple-element.48), kind=kOutput, calls=%fused_computation.29 | convolution fusion | flops 271581184 | bytes 10518528 | tf_op jit(solution)/shard_map/gchqk,gckhd->gcqhd/dot_general | solution.py:42
  97.3 4.7 %all-to-all-start.1 = ((f32[8,1,128,1024]{2,3,1,0:T(8,128)}), f32[8,1,128,1024]{2,3,1,0:T(8,128)}, u32[]{:S(2)}, u32[]{:S(2)}) async-start(f32[8,1,128,1024]{2,3,1,0:T(8,128)} %bitcast.110), calls=%async_computation.1 | async-start | bytes 8388608 | tf_op jit(solution)/shard_map/all_to_all | solution.py:142
  102.1 1.6 gather_fusion
  103.7 2.5 fusion.24
  106.4 4.6 %collective-permute-start = (bf16[2,128,1024]{2,1,0:T(8,128)(2,1)S(1)}, bf16[2,128,1024]{2,1,0:T(8,128)(2,1)}, u32[]{:S(2)}, u32[]{:S(2)}) collective-permute-start(bf16[2,128,1024]{2,1,0:T(8,128)(2,1)S(1)} %get-tuple-element.42), channel_id=1, source_target_pairs={{0,2},{2,4},{4,6},{6,8},{8,10},{10,12},{12,14},{1,3},{3,5},{5,7},{... | collective-permute-start | bytes 1572872 | tf_op jit(solution)/shard_map/ppermute | solution.py:20
  114.2 38.1 %collective-permute-done = bf16[2,128,1024]{2,1,0:T(8,128)(2,1)} collective-permute-done((bf16[2,128,1024]{2,1,0:T(8,128)(2,1)S(1)}, bf16[2,128,1024]{2,1,0:T(8,128)(2,1)}, u32[]{:S(2)}, u32[]{:S(2)}) %collective-permute-start) | collective-permute-done | bytes 524320 | tf_op jit(solution)/shard_map/ppermute | solution.py:20
  152.3 2.7 pad_maximum_fusion.1
  155.1 93.3 %all-reduce.3.cloned.1.call-done = bf16[2,2,128,1024]{3,2,0,1:T(8,128)(2,1)} async-done(((bf16[2,2,128,1024]{3,2,0,1:T(8,128)(2,1)}), bf16[2,2,128,1024]{3,2,0,1:T(8,128)(2,1)}) %all-reduce.3.cloned.1.call-update) | async-done | bytes 1048592 | tf_op jit(solution)/shard_map/psum | solution.py:101
  248.4 2.4 pad_maximum_fusion
  250.8 3.8 %gather_fusion.1 = bf16[10,2,128,1024]{3,2,1,0:T(8,128)(2,1)} fusion(bf16[2,6,128,1024]{3,2,1,0:T(8,128)(2,1)S(1)} %pad_maximum_fusion, s32[1024]{0:T(1024)S(1)} %pad_clamp_fusion.3), kind=kCustom, calls=%fused_computation.1 | custom fusion | bytes 10485800 | tf_op jit(solution)/shard_map/while/body/eval_jaxpr/jit(_take)/gather | solution.py:165
  254.6 8.0 %copy.182 = bf16[2,5,2,128,1024]{3,4,1,0,2:T(8,128)(2,1)} copy(bf16[2,5,2,128,1024]{4,3,2,1,0:T(8,128)(2,1)} %bitcast.109) | data formatting | bytes 10485760 | tf_op jit(solution)/shard_map/while/body/eval_jaxpr/jit(_take)/gather | solution.py:165
  262.6 3.1 %select_bitcast_fusion = bf16[2,2,5,128,1024]{3,4,2,1,0:T(8,128)(2,1)S(1)} fusion(bf16[2,5,2,128,1024]{3,4,1,0,2:T(8,128)(2,1)} %copy.182, pred[2,5]{1,0:T(4,128)(4,1)S(1)} %compare_and_fusion.4), kind=kLoop, calls=%fused_computation.13 | loop fusion | flops 2621440 | bytes 10485770 | tf_op jit(solution)/shard_map/while/body/eval_jaxpr/jit(_take)/select_n | solution.py:165
  269.5 3.2 %fusion.12 = f32[2,5,128,8,128]{2,4,3,1,0:T(8,128)} fusion(bf16[2,5,128,8,128]{2,4,3,1,0:T(8,128)(2,1)S(1)} %bitcast.114, bf16[2,5,8,128,128]{3,4,1,2,0:T(8,128)(2,1)S(1)} %get-tuple-element.26), kind=kOutput, calls=%fused_computation.27 | convolution fusion | flops 335544320 | bytes 10485760 | tf_op jit(solution)/shard_map/while/body/eval_jaxpr/gchqk,gckhd->gcqhd/dot_general | solution.py:42
  274.1 2.9 gather_fusion.4
  277.0 3.2 %fusion.1 = f32[2,128,8,128]{1,3,2,0:T(8,128)S(1)} fusion(f32[2,3,128,8,128]{2,4,3,1,0:T(8,128)S(1)} %bitcast.113, f32[2,5,128,8,128]{2,4,3,1,0:T(8,128)} %fusion.12, f32[2,8,128,8]{2,3,1,0:T(8,128)S(1)} %copy.207), kind=kLoop, calls=%fused_computation.9 | loop fusion | flops 6029312 | bytes 9502720 | tf_op jit(solution)/shard_map/while/body/eval_jaxpr/reduce_sum | solution.py:56
  281.6 8.8 %all-gather.2.cloned.1.call-done = bf16[256,2048]{1,0:T(8,128)(2,1)} async-done(((bf16[256,1024]{1,0:T(8,128)(2,1)}), bf16[256,2048]{1,0:T(8,128)(2,1)}) %all-gather.2.cloned.1.call-update) | async-done | bytes 1048592 | tf_op jit(solution)/shard_map/all_gather | solution.py:178
  290.4 4.6 %convolution_convert_fusion = bf16[256,1024]{1,0:T(8,128)(2,1)} fusion(bf16[256,2048]{1,0:T(8,128)(2,1)} %all-gather.2.cloned.1.call-done, bf16[2048,1024]{1,0:T(8,128)(2,1)} %param.10), kind=kOutput, calls=%fused_computation.36 | convolution fusion | flops 1074003968 | bytes 5767168 | tf_op jit(solution)/shard_map/dot_general | solution.py:177
  (85 shorter events, 13.8 us)
Async XLA Ops:
  10.1 9.5 %copy-start.1 = (bf16[256,1024]{1,0:T(8,128)(2,1)S(1)}, bf16[256,1024]{1,0:T(8,128)(2,1)}, u32[]{:S(2)}) copy-start(bf16[256,1024]{1,0:T(8,128)(2,1)} %param.9) | copy-start | bytes 1572868
  10.1 9.5 %copy-start.3 = (bf16[256,1024]{1,0:T(8,128)(2,1)S(1)}, bf16[256,1024]{1,0:T(8,128)(2,1)}, u32[]{:S(2)}) copy-start(bf16[256,1024]{1,0:T(8,128)(2,1)} %param.8) | copy-start | bytes 1572868
  11.7 55.7 %all-to-all-start = ((bf16[8,1,128,1024]{3,2,1,0:T(8,128)(2,1)}), bf16[8,1,128,1024]{3,2,1,0:T(8,128)(2,1)}, u32[]{:S(2)}, u32[]{:S(2)}) async-start(bf16[8,1,128,1024]{3,2,1,0:T(8,128)(2,1)} %fusion.18), calls=%async_computation | async-start | bytes 4194304 | tf_op jit(solution)/shard_map/all_to_all | solution.py:137
  77.0 10.3 %all-to-all-start.2 = ((f32[8,1,128,8]{2,3,1,0:T(8,128)}), f32[8,1,128,8]{2,3,1,0:T(8,128)S(1)}, u32[]{:S(2)}, u32[]{:S(2)}) async-start(f32[8,1,128,8]{2,3,1,0:T(8,128)} %bitcast.39), calls=%async_computation.2 | async-start | bytes 65536 | tf_op jit(solution)/shard_map/all_to_all | solution.py:143
  87.3 10.0 %all-to-all-start.3 = ((f32[8,1,128,8]{2,3,1,0:T(8,128)}), f32[8,1,128,8]{2,3,1,0:T(8,128)S(1)}, u32[]{:S(2)}, u32[]{:S(2)}) async-start(f32[8,1,128,8]{2,3,1,0:T(8,128)} %bitcast.44), calls=%async_computation.3 | async-start | bytes 65536 | tf_op jit(solution)/shard_map/all_to_all | solution.py:144
  97.3 4.8 %copy-start.6 = (s32[2]{0:T(128)S(1)}, s32[2]{0:T(128)}, u32[]{:S(2)}) copy-start(s32[2]{0:T(128)} %param.13) | copy-start | bytes 28
  97.3 176.8 %all-to-all-start.1 = ((f32[8,1,128,1024]{2,3,1,0:T(8,128)}), f32[8,1,128,1024]{2,3,1,0:T(8,128)}, u32[]{:S(2)}, u32[]{:S(2)}) async-start(f32[8,1,128,1024]{2,3,1,0:T(8,128)} %bitcast.110), calls=%async_computation.1 | async-start | bytes 8388608 | tf_op jit(solution)/shard_map/all_to_all | solution.py:142
  102.0 4.4 %copy-start.2 = (bf16[256,1024]{1,0:T(8,128)(2,1)S(1)}, bf16[256,1024]{1,0:T(8,128)(2,1)}, u32[]{:S(2)}) copy-start(bf16[256,1024]{1,0:T(8,128)(2,1)} %param.9) | copy-start | bytes 1572868
  102.0 4.3 %copy-start.4 = (bf16[256,1024]{1,0:T(8,128)(2,1)S(1)}, bf16[256,1024]{1,0:T(8,128)(2,1)}, u32[]{:S(2)}) copy-start(bf16[256,1024]{1,0:T(8,128)(2,1)} %param.8) | copy-start | bytes 1572868
  102.0 10.8 %copy-start.7 = (s32[2]{0:T(128)S(1)}, s32[2]{0:T(128)}, u32[]{:S(2)}) copy-start(s32[2]{0:T(128)} %param.12) | copy-start | bytes 28
  102.0 11.3 %copy-start = (bf16[256,1024]{1,0:T(8,128)(2,1)S(1)}, bf16[256,1024]{1,0:T(8,128)(2,1)}, u32[]{:S(2)}) copy-start(bf16[256,1024]{1,0:T(8,128)(2,1)} %param.7) | copy-start | bytes 1572868
  102.0 146.3 %all-reduce.3.cloned.1.call-start = ((), (), s32[]{:S(2)}) async-start(), calls=%async_computation.4 | async-start | bytes 2097152 | tf_op jit(solution)/shard_map/psum | solution.py:101
  106.3 184.1 %all-gather.2.cloned.1.call-start = ((), (), s32[]{:S(2)}) async-start(), calls=%async_computation.5 | async-start | bytes 1572864 | tf_op jit(solution)/shard_map/all_gather | solution.py:178
  106.4 45.9 %collective-permute-start = (bf16[2,128,1024]{2,1,0:T(8,128)(2,1)S(1)}, bf16[2,128,1024]{2,1,0:T(8,128)(2,1)}, u32[]{:S(2)}, u32[]{:S(2)}) collective-permute-start(bf16[2,128,1024]{2,1,0:T(8,128)(2,1)S(1)} %get-tuple-element.42), channel_id=1, source_target_pairs={{0,2},{2,4},{4,6},{6,8},{8,10},{10,12},{12,14},{1,3},{3,5},{5,7},{... | collective-permute-start | bytes 1572872 | tf_op jit(solution)/shard_map/ppermute | solution.py:20
  111.0 41.3 %collective-permute-start.1 = (bf16[2,128,1024]{2,1,0:T(8,128)(2,1)S(1)}, bf16[2,128,1024]{2,1,0:T(8,128)(2,1)}, u32[]{:S(2)}, u32[]{:S(2)}) collective-permute-start(bf16[2,128,1024]{2,1,0:T(8,128)(2,1)S(1)} %get-tuple-element.43), channel_id=1, source_target_pairs={{2,0},{4,2},{6,4},{8,6},{10,8},{12,10},{14,12},{3,1},{5,3},{7,5},{... | collective-permute-start | bytes 1572872 | tf_op jit(solution)/shard_map/ppermute | solution.py:23
  265.7 1.0 copy-start.5
Sparse Core Ops, SparseCore 0:
  106.4 141.9 all-reduce.2
  281.7 8.6 all-gather.1
where the time goes:
time: 303 us; the launch traced here: 302 us
  waiting for transfers between devices  180 us (59%)
  local copies, waits for them, and re-layouts  37.8 us (12%)
  other arithmetic  25.6 us (8%)
  starting transfers between devices  25.1 us (8%)
  matrix products  19.7 us (7%)
  between operations  13.8 us (5%)
    psum x1, waiting for transfers between devices, per_device(): global_pairs = lax.psum(global_terms.astype(jnp.bfloat16), 'ctx')  93.3 us
    ppermute x1, waiting for transfers between devices, with_halo(): lax.ppermute(lax.slice_in_dim(block, block.shape[dim] - width, None, axis...  38.1 us
    all_to_all x1, waiting for transfers between devices, per_device(): lax.all_to_all(outgoing, 'ctx', split_axis=0, concat_axis=0, tiled=True)  35 us
    gather x2, local copies, waits for them, and re-layouts, attend(): gathered = jnp.take(local_pool, index_group, axis=1)  11.8 us
    all_gather x1, waiting for transfers between devices, per_device(): lax.all_gather(attended, 'head', axis=1, tiled=True)  8.78 us
    dot_general x2, matrix products, block_partial(): jnp.einsum('gchqk,gckhd->gcqhd', weights.astype(jnp.bfloat16), value_head...  8.28 us
    all_to_all x1, starting transfers between devices, per_device(): lax.all_to_all(outgoing, 'ctx', split_axis=0, concat_axis=0, tiled=True)  7.31 us
    dot_general x2, matrix products, block_partial(): jnp.einsum('gqhd,gckhd->gchqk', query_heads, key_heads, preferred_element...  6.82 us
  transfers between devices with their start and end apart: 8, of which 6 were waited for; matrix products, arithmetic and copies ran while one was open for 18% of the time, Pallas kernels for 0%

commit v1 on v0

--- a/solution.py
+++ b/solution.py
@@ -98,7 +98,8 @@
     picked = jnp.take(own_blocks, global_slot, axis=1)
     owned_here = (global_owner == position)[None, :, None, None]
     global_terms = jnp.where(owned_here, picked.astype(jnp.float32), 0.0)
-    global_pairs = lax.psum(global_terms.astype(jnp.bfloat16), "ctx")
+    in_array = global_terms.astype(jnp.bfloat16)
+    global_pairs = lax.all_gather(in_array, "ctx").sum(axis=0)
     request_table = random_blocks.reshape(ctx_count, requests)
     owners = request_table // dev_blocks
     within = request_table % dev_blocks

time: 303 us -> 337 us (1.11)
  waiting for transfers between devices: 180 us -> 204 us
  other arithmetic: 25.6 us -> 31.3 us
  local copies, waits for them, and re-layouts: 37.8 us -> 43.3 us
    psum x1 -> x0, waiting for transfers between devices: 93.3 us -> none  [per_device(): global_pairs = lax.psum(global_terms.astype(jnp.bfloat16), 'ctx')]
    all_to_all x1, waiting for transfers between devices: 0.01 us -> 68 us  [per_device(): lax.all_to_all(part_out, 'ctx', split_axis=0, concat_axis=0, tiled=True)]
    all_to_all x1, waiting for transfers between devices: 35 us -> 64.5 us  [per_device(): lax.all_to_all(outgoing, 'ctx', split_axis=0, concat_axis=0, tiled=True)]
    all_gather x1, waiting for transfers between devices: 8.78 us -> 21.9 us  [per_device(): lax.all_gather(attended, 'head', axis=1, tiled=True)]
    reduce_sum x0 -> x1, other arithmetic: none -> 6.77 us  [per_device(): global_pairs = lax.all_gather(in_array, 'ctx').sum(axis=0)]
    ppermute x1, waiting for transfers between devices: 38.1 us -> 44.2 us  [with_halo(): lax.ppermute(lax.slice_in_dim(block, block.shape[dim] - width, None, axis...]
  transfers between devices with their start and end apart: 8 -> 8, of which waited for: 6 -> 6; matrix products, arithmetic and copies ran while one was open for 18% -> 15% of each run, Pallas kernels for 0% -> 0%
where the time goes in v1:
time: 337 us; the launch traced here: 336 us
  waiting for transfers between devices  204 us (61%)
  local copies, waits for them, and re-layouts  43.3 us (13%)
  other arithmetic  31.3 us (9%)
  starting transfers between devices  25.8 us (8%)
  matrix products  18.1 us (5%)
  between operations  13.7 us (4%)
    all_to_all x1, waiting for transfers between devices, per_device(): lax.all_to_all(part_out, 'ctx', split_axis=0, concat_axis=0, tiled=True)  68 us
    all_to_all x1, waiting for transfers between devices, per_device(): lax.all_to_all(outgoing, 'ctx', split_axis=0, concat_axis=0, tiled=True)  64.5 us
    ppermute x1, waiting for transfers between devices, with_halo(): lax.ppermute(lax.slice_in_dim(block, block.shape[dim] - width, None, axis...  44.2 us
    all_gather x1, waiting for transfers between devices, per_device(): lax.all_gather(attended, 'head', axis=1, tiled=True)  21.9 us
    gather x2, local copies, waits for them, and re-layouts, attend(): gathered = jnp.take(local_pool, index_group, axis=1)  11.7 us
    all_to_all x1, starting transfers between devices, per_device(): lax.all_to_all(outgoing, 'ctx', split_axis=0, concat_axis=0, tiled=True)  7.31 us
    dot_general x2, matrix products, block_partial(): jnp.einsum('gqhd,gckhd->gchqk', query_heads, key_heads, preferred_element...  6.92 us
    reduce_sum x1, other arithmetic, per_device(): global_pairs = lax.all_gather(in_array, 'ctx').sum(axis=0)  6.77 us
  transfers between devices with their start and end apart: 8, of which 6 were waited for; matrix products, arithmetic and copies ran while one was open for 15% of the time, Pallas kernels for 0%

profile of v1, /device:TPU:0, one launch (start us, length us, event | category | flops | bytes accessed | tf_op | source)
XLA Modules:
  0.0 336.1 jit_solution(4920446498483114145)
XLA Ops:
  11.8 2.0 gather_fusion.3
  13.8 3.2 fusion.18
  17.0 7.3 %all-to-all-start = ((bf16[8,1,128,1024]{3,2,1,0:T(8,128)(2,1)}), bf16[8,1,128,1024]{3,2,1,0:T(8,128)(2,1)}, u32[]{:S(2)}, u32[]{:S(2)}) async-start(bf16[8,1,128,1024]{3,2,1,0:T(8,128)(2,1)} %fusion.18), calls=%async_computation | async-start | bytes 4194304 | tf_op jit(solution)/shard_map/all_to_all | solution.py:138
  24.9 2.8 gather_fusion.2
  27.6 2.7 bitcast_select_fusion
  30.3 2.5 fusion.47
  32.7 3.9 %copy.179 = bf16[1,8,1,128,1024]{3,4,1,2,0:T(8,128)(2,1)} copy(bf16[1,8,1,128,1024]{4,3,0,1,2:T(8,128)(2,1)} %get-tuple-element.40) | data formatting | bytes 4194304 | tf_op jit(solution)/shard_map/slice | solution.py:142
  36.7 3.9 %copy.178 = bf16[1,8,1,128,1024]{3,4,1,2,0:T(8,128)(2,1)} copy(bf16[1,8,1,128,1024]{4,3,0,1,2:T(8,128)(2,1)} %get-tuple-element.41) | data formatting | bytes 4194304 | tf_op jit(solution)/shard_map/slice | solution.py:142
  40.6 64.5 %all-to-all-done = bf16[8,1,128,1024]{3,2,1,0:T(8,128)(2,1)} async-done(((bf16[8,1,128,1024]{3,2,1,0:T(8,128)(2,1)}), bf16[8,1,128,1024]{3,2,1,0:T(8,128)(2,1)}, u32[]{:S(2)}, u32[]{:S(2)}) %all-to-all-start) | async-done | bytes 2097184 | tf_op jit(solution)/shard_map/all_to_all | solution.py:138
  105.1 4.0 %copy.181 = bf16[8,1,128,1024]{2,3,0,1:T(8,128)(2,1)} copy(bf16[8,1,128,1024]{3,2,1,0:T(8,128)(2,1)} %all-to-all-done) | data formatting | bytes 4194304 | tf_op jit(solution)/shard_map/all_to_all | solution.py:138
  109.1 5.7 %bitcast_reduce_fusion.1 = (f32[8,8,128]{2,1,0:T(8,128)}, f32[8,8,128,128]{3,2,1,0:T(8,128)}) fusion(bf16[8,128,8,128]{1,3,2,0:T(8,128)(2,1)} %bitcast.122, bf16[8,128,8,128]{1,3,2,0:T(8,128)(2,1)} %bitcast.123), kind=kOutput, calls=%fused_computation.18 | convolution fusion | flops 270524416 | bytes 8421376 | tf_op jit(solution)/shard_map/gqhd,gckhd->gchqk/dot_general | solution.py:36
  114.8 3.4 %all-to-all-start.2 = ((f32[8,1,128,8]{2,3,1,0:T(8,128)}), f32[8,1,128,8]{2,3,1,0:T(8,128)S(1)}, u32[]{:S(2)}, u32[]{:S(2)}) async-start(f32[8,1,128,8]{2,3,1,0:T(8,128)} %bitcast.40), calls=%async_computation.2 | async-start | bytes 65536 | tf_op jit(solution)/shard_map/all_to_all | solution.py:144
  118.3 3.7 %fusion.6 = f32[8,8,128]{2,1,0:T(8,128)} fusion(f32[8,8,128,128]{3,2,1,0:T(8,128)} %get-tuple-element.49, f32[8,8,128]{2,1,0:T(8,128)} %get-tuple-element.48), kind=kLoop, calls=%fused_computation.20 | loop fusion | flops 3137536 | bytes 4259840 | tf_op jit(solution)/shard_map/reduce_sum | solution.py:41
  122.0 3.6 %all-to-all-done.2 = f32[8,1,128,8]{2,3,1,0:T(8,128)S(1)} async-done(((f32[8,1,128,8]{2,3,1,0:T(8,128)}), f32[8,1,128,8]{2,3,1,0:T(8,128)S(1)}, u32[]{:S(2)}, u32[]{:S(2)}) %all-to-all-start.2) | async-done | bytes 32800 | tf_op jit(solution)/shard_map/all_to_all | solution.py:144
  125.6 4.3 %all-to-all-start.3 = ((f32[8,1,128,8]{2,3,1,0:T(8,128)}), f32[8,1,128,8]{2,3,1,0:T(8,128)S(1)}, u32[]{:S(2)}, u32[]{:S(2)}) async-start(f32[8,1,128,8]{2,3,1,0:T(8,128)} %bitcast.45), calls=%async_computation.3 | async-start | bytes 65536 | tf_op jit(solution)/shard_map/all_to_all | solution.py:145
  129.9 5.8 %fusion.16 = f32[8,8,128,128]{3,2,1,0:T(8,128)} fusion(bf16[8,128,8,128]{1,3,2,0:T(8,128)(2,1)} %bitcast.120, f32[8,8,128,128]{3,2,1,0:T(8,128)} %get-tuple-element.49, f32[8,8,128]{2,1,0:T(8,128)} %get-tuple-element.48), kind=kOutput, calls=%fused_computation.29 | convolution fusion | flops 271581184 | bytes 10518528 | tf_op jit(solution)/shard_map/gchqk,gckhd->gcqhd/dot_general | solution.py:42
  135.7 1.6 all-to-all-done.3
  137.3 4.7 %all-to-all-start.1 = ((f32[8,1,128,1024]{2,3,1,0:T(8,128)}), f32[8,1,128,1024]{2,3,1,0:T(8,128)}, u32[]{:S(2)}, u32[]{:S(2)}) async-start(f32[8,1,128,1024]{2,3,1,0:T(8,128)} %bitcast.114), calls=%async_computation.1 | async-start | bytes 8388608 | tf_op jit(solution)/shard_map/all_to_all | solution.py:143
  142.1 4.6 %collective-permute-start = (bf16[2,128,1024]{2,1,0:T(8,128)(2,1)S(1)}, bf16[2,128,1024]{2,1,0:T(8,128)(2,1)}, u32[]{:S(2)}, u32[]{:S(2)}) collective-permute-start(bf16[2,128,1024]{2,1,0:T(8,128)(2,1)S(1)} %get-tuple-element.42), channel_id=1, source_target_pairs={{0,2},{2,4},{4,6},{6,8},{8,10},{10,12},{12,14},{1,3},{3,5},{5,7},{... | collective-permute-start | bytes 1572872 | tf_op jit(solution)/shard_map/ppermute | solution.py:20
  146.7 1.5 collective-permute-start.1
  149.9 44.2 %collective-permute-done = bf16[2,128,1024]{2,1,0:T(8,128)(2,1)} collective-permute-done((bf16[2,128,1024]{2,1,0:T(8,128)(2,1)S(1)}, bf16[2,128,1024]{2,1,0:T(8,128)(2,1)}, u32[]{:S(2)}, u32[]{:S(2)}) %collective-permute-start) | collective-permute-done | bytes 524320 | tf_op jit(solution)/shard_map/ppermute | solution.py:20
  194.1 2.7 pad_maximum_fusion.1
  198.0 68.0 %all-to-all-done.1 = f32[8,1,128,1024]{2,3,1,0:T(8,128)} async-done(((f32[8,1,128,1024]{2,3,1,0:T(8,128)}), f32[8,1,128,1024]{2,3,1,0:T(8,128)}, u32[]{:S(2)}, u32[]{:S(2)}) %all-to-all-start.1) | async-done | bytes 4194336 | tf_op jit(solution)/shard_map/all_to_all | solution.py:143
  266.0 4.6 %gather_fusion.4 = f32[6,128,1024]{1,2,0:T(8,128)} fusion(f32[8,128,1024]{1,2,0:T(8,128)} %bitcast.35, s32[1024]{0:T(1024)S(1)} %pad_clamp_fusion), kind=kCustom, calls=%fused_computation.4 | custom fusion | bytes 6291480 | tf_op jit(solution)/shard_map/gather | solution.py:147
  270.6 6.8 %reduce_sum.91 = bf16[2,2,128,1024]{3,2,1,0:T(8,128)(2,1)} reduce(bf16[8,2,2,128,1024]{4,3,2,1,0:T(8,128)(2,1)} %all-gather.3.cloned.1.call-done, bf16[]{:T(256)} %constant.162.clone.1), dimensions={0}, to_apply=%region_0.1 | reduce | flops 3670016 | bytes 9437186 | tf_op jit(solution)/shard_map/reduce_sum | solution.py:102
  277.3 2.2 pad_maximum_fusion
  279.5 3.8 %gather_fusion.1 = bf16[10,2,128,1024]{3,2,1,0:T(8,128)(2,1)} fusion(bf16[2,6,128,1024]{3,2,1,0:T(8,128)(2,1)S(1)} %pad_maximum_fusion, s32[1024]{0:T(1024)S(1)} %pad_clamp_fusion.3), kind=kCustom, calls=%fused_computation.1 | custom fusion | bytes 10485800 | tf_op jit(solution)/shard_map/while/body/eval_jaxpr/jit(_take)/gather | solution.py:166
  283.4 7.9 %copy.163 = bf16[2,5,2,128,1024]{3,4,1,0,2:T(8,128)(2,1)} copy(bf16[2,5,2,128,1024]{4,3,2,1,0:T(8,128)(2,1)} %bitcast.113) | data formatting | bytes 10485760 | tf_op jit(solution)/shard_map/while/body/eval_jaxpr/jit(_take)/gather | solution.py:166
  291.3 3.1 select_bitcast_fusion
  296.5 1.5 fusion.3
  302.9 21.9 %all-gather.5.cloned.1.call-done = bf16[256,2048]{1,0:T(8,128)(2,1)} async-done(((bf16[256,1024]{1,0:T(8,128)(2,1)}), bf16[256,2048]{1,0:T(8,128)(2,1)}) %all-gather.5.cloned.1.call-update) | async-done | bytes 1048592 | tf_op jit(solution)/shard_map/all_gather | solution.py:179
  324.7 4.6 %convolution_convert_fusion = bf16[256,1024]{1,0:T(8,128)(2,1)} fusion(bf16[256,2048]{1,0:T(8,128)(2,1)} %all-gather.5.cloned.1.call-done, bf16[2048,1024]{1,0:T(8,128)(2,1)} %param.10), kind=kOutput, calls=%fused_computation.36 | convolution fusion | flops 1074003968 | bytes 5767168 | tf_op jit(solution)/shard_map/dot_general | solution.py:178
  (86 shorter events, 15.6 us)
Async XLA Ops:
  6.5 264.0 %all-gather.3.cloned.1.call-start = ((), (), s32[]{:S(2)}) async-start(), calls=%async_computation.4 | async-start | bytes 9437184 | tf_op jit(solution)/shard_map/all_gather | solution.py:102
  8.5 2.1 copy-start.5
  8.5 3.3 copy-start
  17.0 88.1 %all-to-all-start = ((bf16[8,1,128,1024]{3,2,1,0:T(8,128)(2,1)}), bf16[8,1,128,1024]{3,2,1,0:T(8,128)(2,1)}, u32[]{:S(2)}, u32[]{:S(2)}) async-start(bf16[8,1,128,1024]{3,2,1,0:T(8,128)(2,1)} %fusion.18), calls=%async_computation | async-start | bytes 4194304 | tf_op jit(solution)/shard_map/all_to_all | solution.py:138
  114.8 10.7 %all-to-all-start.2 = ((f32[8,1,128,8]{2,3,1,0:T(8,128)}), f32[8,1,128,8]{2,3,1,0:T(8,128)S(1)}, u32[]{:S(2)}, u32[]{:S(2)}) async-start(f32[8,1,128,8]{2,3,1,0:T(8,128)} %bitcast.40), calls=%async_computation.2 | async-start | bytes 65536 | tf_op jit(solution)/shard_map/all_to_all | solution.py:144
  125.6 11.7 %all-to-all-start.3 = ((f32[8,1,128,8]{2,3,1,0:T(8,128)}), f32[8,1,128,8]{2,3,1,0:T(8,128)S(1)}, u32[]{:S(2)}, u32[]{:S(2)}) async-start(f32[8,1,128,8]{2,3,1,0:T(8,128)} %bitcast.45), calls=%async_computation.3 | async-start | bytes 65536 | tf_op jit(solution)/shard_map/all_to_all | solution.py:145
  137.2 4.8 %copy-start.2 = (bf16[256,1024]{1,0:T(8,128)(2,1)S(1)}, bf16[256,1024]{1,0:T(8,128)(2,1)}, u32[]{:S(2)}) copy-start(bf16[256,1024]{1,0:T(8,128)(2,1)} %param.9) | copy-start | bytes 1572868
  137.3 4.8 %copy-start.3 = (bf16[256,1024]{1,0:T(8,128)(2,1)S(1)}, bf16[256,1024]{1,0:T(8,128)(2,1)}, u32[]{:S(2)}) copy-start(bf16[256,1024]{1,0:T(8,128)(2,1)} %param.8) | copy-start | bytes 1572868
  137.3 10.9 %copy-start.6 = (s32[2]{0:T(128)S(1)}, s32[2]{0:T(128)}, u32[]{:S(2)}) copy-start(s32[2]{0:T(128)} %param.13) | copy-start | bytes 28
  137.3 11.2 %copy-start.7 = (s32[2]{0:T(128)S(1)}, s32[2]{0:T(128)}, u32[]{:S(2)}) copy-start(s32[2]{0:T(128)} %param.12) | copy-start | bytes 28
  137.3 128.7 %all-to-all-start.1 = ((f32[8,1,128,1024]{2,3,1,0:T(8,128)}), f32[8,1,128,1024]{2,3,1,0:T(8,128)}, u32[]{:S(2)}, u32[]{:S(2)}) async-start(f32[8,1,128,1024]{2,3,1,0:T(8,128)} %bitcast.114), calls=%async_computation.1 | async-start | bytes 8388608 | tf_op jit(solution)/shard_map/all_to_all | solution.py:143
  142.0 182.8 %all-gather.5.cloned.1.call-start = ((), (), s32[]{:S(2)}) async-start(), calls=%async_computation.5 | async-start | bytes 1572864 | tf_op jit(solution)/shard_map/all_gather | solution.py:179
  142.1 52.0 %collective-permute-start = (bf16[2,128,1024]{2,1,0:T(8,128)(2,1)S(1)}, bf16[2,128,1024]{2,1,0:T(8,128)(2,1)}, u32[]{:S(2)}, u32[]{:S(2)}) collective-permute-start(bf16[2,128,1024]{2,1,0:T(8,128)(2,1)S(1)} %get-tuple-element.42), channel_id=1, source_target_pairs={{0,2},{2,4},{4,6},{6,8},{8,10},{10,12},{12,14},{1,3},{3,5},{5,7},{... | collective-permute-start | bytes 1572872 | tf_op jit(solution)/shard_map/ppermute | solution.py:20
  146.7 47.4 %collective-permute-start.1 = (bf16[2,128,1024]{2,1,0:T(8,128)(2,1)S(1)}, bf16[2,128,1024]{2,1,0:T(8,128)(2,1)}, u32[]{:S(2)}, u32[]{:S(2)}) collective-permute-start(bf16[2,128,1024]{2,1,0:T(8,128)(2,1)S(1)} %get-tuple-element.43), channel_id=1, source_target_pairs={{2,0},{4,2},{6,4},{8,6},{10,8},{12,10},{14,12},{3,1},{5,3},{7,5},{... | collective-permute-start | bytes 1572872 | tf_op jit(solution)/shard_map/ppermute | solution.py:23
  294.3 1.0 copy-start.4
  298.3 1.9 copy-start.1
Sparse Core Ops, SparseCore 0:
  10.8 234.3 all-gather.2
  303.0 21.7 all-gather.4
